TPU v7x, 32 devices: a whole 2x2x4 slice. The times are simulated.
32 devices in a mesh: ctx: 16 (over z, y, core), head: 2 (over x).
Axes of the slice: x: 2, y: 2, z: 4, core: 2. Of those that a mesh axis runs over, the one named last changes fastest.
Arguments:
- queries: bfloat16 [2048, 8192], P('ctx', 'head'), may hold values from -5.5 to 5.5
- keys: bfloat16 [2048, 1024], P('ctx', 'head'), may hold values from -5.5 to 5.5
- values: bfloat16 [2048, 1024], P('ctx', 'head'), may hold values from -6 to 6
- feature_weights: bfloat16 [64, 128, 64], P('head'), may hold values from -1 to 1
Outputs:
- attn_error: float32 [2048, 8192], P('ctx', 'head')
- loss: float32 [], replicated
- grad_w: float32 [64, 128, 64], P('head')
All inputs are finite; a program needn't handle non-finite values.
Results may differ from a plain program's by a relative error of at most 0.004.
Values may be sent and summed in bfloat16 or wider, within the bound.
No kernel may reach another device: no remote copies, remote signals or barrier semaphores. Data moves between devices by JAX's collectives and lax.ppermute only.
A program may use at most 192 MiB of HBM per device.

v0:
```python
import math
import jax
import jax.numpy as jnp
from jax import lax
from jax.sharding import PartitionSpec as P

HEAD_SIZE = 128
QUERY_HEADS = 64
KEY_VALUE_HEADS = 8
FM = 64
WIN = 64
phi_scale = 0.00390625
big_negative = -1e30
highest = lax.Precision.HIGHEST


def swapped(value, axis, distance):
    mask = 2**distance
    pairs = [(source, source ^ mask) for source in range(lax.axis_size(axis))]
    return lax.ppermute(value, axis, pairs)


def carried_in(value, axis, combine, identity):
    devices, here = (lax.axis_size(axis), lax.axis_index(axis))
    everything = jax.tree.map(
        lambda part, kind: lax.all_gather(part.astype(kind), axis),
        value,
        (jnp.bfloat16, jnp.bfloat16),
    )
    start = jax.tree.map(
        lambda part, zero: jnp.broadcast_to(jnp.asarray(zero, part.dtype), part.shape),
        value,
        identity,
    )

    def carried_step(k, before):
        reached = k < here
        new = combine(
            before, jax.tree.map(lambda part, own: part[k].astype(own.dtype), everything, value)
        )
        return jax.tree.map(lambda a, b: jnp.where(reached, a, b), new, before)

    return lax.fori_loop(0, devices, carried_step, start)


def prefix(value, axis, combine, identity):
    devices, here = (lax.axis_size(axis), lax.axis_index(axis))
    everything = jax.tree.map(
        lambda part, kind: lax.all_gather(part.astype(kind), axis),
        value,
        jax.tree.map(lambda a: jnp.bfloat16 if a.dtype == jnp.float32 else a.dtype, value),
    )
    start = jax.tree.map(
        lambda part, zero: jnp.broadcast_to(jnp.asarray(zero, part.dtype), part.shape),
        value,
        identity,
    )

    def prefix_step(k, before):
        at = devices - 1 - k
        reached = at > here
        new = combine(
            before, jax.tree.map(lambda part, own: part[at].astype(own.dtype), everything, value)
        )
        return jax.tree.map(lambda a, b: jnp.where(reached, a, b), new, before)

    return lax.fori_loop(0, devices, prefix_step, start)


def features(projection):
    return phi_scale * jnp.concatenate(
        [1.0 + jax.nn.elu(projection), 1.0 + jax.nn.elu(-projection)], axis=-1
    )


def feature_back(projection, grad_phi):
    half = projection.shape[-1]
    slope_plus = jnp.where(projection > 0, 1.0, jnp.exp(jnp.minimum(projection, 0.0)))
    slope_minus = jnp.where(projection < 0, 1.0, jnp.exp(jnp.minimum(-projection, 0.0)))
    return phi_scale * (grad_phi[..., :half] * slope_plus - grad_phi[..., half:] * slope_minus)


def add_pair(earlier, later):
    return (earlier[0] + later[0], earlier[1] + later[1])


def split_product(form, phi_part, data):
    upper = phi_part.astype(jnp.bfloat16)
    lower = (phi_part - upper.astype(jnp.float32)).astype(jnp.bfloat16)
    return jnp.einsum(form, upper, data, preferred_element_type=jnp.float32) + jnp.einsum(
        form, lower, data, preferred_element_type=jnp.float32
    )


def visit_partner(rows):
    for bit_index in range(lax.axis_size("ctx").bit_length() - 1):
        rows = swapped(rows, "ctx", bit_index)
    return rows


def return_partner(rows):
    for bit_index in range(lax.axis_size("ctx").bit_length() - 1):
        rows = swapped(rows.astype(jnp.bfloat16), "ctx", bit_index).astype(rows.dtype)
    return rows


def teacher_part(part, query_set, pos_set, key_block, value_block, key_pos, masked):
    scale_factor = 1.0 / math.sqrt(query_set.shape[-1])
    scores = (
        jnp.einsum("qgrd,kgd->grqk", query_set, key_block, preferred_element_type=jnp.float32)
        * scale_factor
    )
    if masked:
        causal = key_pos[None, :] <= pos_set[:, None]
        top = jnp.maximum(part[0], jnp.max(jnp.where(causal, scores, big_negative), axis=-1))
        weights = jnp.exp(jnp.where(causal, scores - top[..., None], big_negative))
    else:
        top = jnp.maximum(part[0], jnp.max(scores, axis=-1))
        weights = jnp.exp(scores - top[..., None])
    rescale = jnp.exp(part[0] - top)
    total = part[1] * rescale + jnp.sum(weights, axis=-1)
    mixed = part[2] * rescale[..., None] + jnp.einsum(
        "grqk,kgd->grqd",
        weights.astype(jnp.bfloat16),
        value_block,
        preferred_element_type=jnp.float32,
    )
    return (top, total, mixed)


def advance(part, row_set, key_block, value_block, key_pos, first):
    query_set, pos_set = row_set
    needed = first <= pos_set[-1]
    straddle = key_pos[-1] > pos_set[0]
    branch_index = jnp.where(needed, jnp.where(straddle, 2, 1), 0).astype(jnp.int32)
    return lax.switch(
        branch_index,
        [
            lambda current: current,
            lambda current: teacher_part(
                current, query_set, pos_set, key_block, value_block, key_pos, False
            ),
            lambda current: teacher_part(
                current, query_set, pos_set, key_block, value_block, key_pos, True
            ),
        ],
        part,
    )


def shards(queries, keys, values, feature_weights):
    local_rows = queries.shape[0]
    half_rows = local_rows // 2
    groups = keys.shape[1] // HEAD_SIZE
    group_ratio = QUERY_HEADS // KEY_VALUE_HEADS
    heads_here = groups * group_ratio
    ctx_count = lax.axis_size("ctx")
    ctx_place = lax.axis_index("ctx")
    own_start = ctx_place * local_rows
    query4 = queries.reshape(local_rows, groups, group_ratio, HEAD_SIZE)
    own_keys = keys.reshape(local_rows, groups, HEAD_SIZE)
    own_values = values.reshape(local_rows, groups, HEAD_SIZE)
    weight4 = feature_weights.reshape(groups, group_ratio, HEAD_SIZE, FM)
    scale = 1.0 / math.sqrt(HEAD_SIZE)
    query_pos = own_start + jnp.arange(local_rows, dtype=jnp.int32)
    tail_offsets = jnp.arange(WIN, dtype=jnp.int32)
    proj_own = jnp.einsum("kgd,grdf->grkf", own_keys, weight4, preferred_element_type=jnp.float32)
    first_set = (query4[:half_rows], query_pos[:half_rows])
    partner_start = (ctx_count - 1 - ctx_place) * local_rows
    visiting = visit_partner(query4[half_rows:])
    second_set = (visiting, partner_start + half_rows + jnp.arange(half_rows, dtype=jnp.int32))
    row_sets = (first_set, second_set)

    def add_tail(tails, key_block, value_block, key_pos):
        pick = (key_pos[None, :] == own_start - WIN + tail_offsets[:, None]).astype(jnp.bfloat16)
        return (
            tails[0]
            + jnp.einsum("wk,kgd->wgd", pick, key_block, preferred_element_type=jnp.float32),
            tails[1]
            + jnp.einsum("wk,kgd->wgd", pick, value_block, preferred_element_type=jnp.float32),
        )

    part_zero = (
        jnp.full((groups, group_ratio, half_rows), big_negative, jnp.float32),
        jnp.zeros((groups, group_ratio, half_rows), jnp.float32),
        jnp.zeros((groups, group_ratio, half_rows, HEAD_SIZE), jnp.float32),
    )
    tail_zero = (
        jnp.zeros((WIN, groups, HEAD_SIZE), jnp.float32),
        jnp.zeros((WIN, groups, HEAD_SIZE), jnp.float32),
    )
    state_zero = (
        jnp.zeros((groups, group_ratio, 2 * FM, HEAD_SIZE), jnp.float32),
        jnp.zeros((groups, group_ratio, 2 * FM), jnp.float32),
    )
    carry = ((part_zero, part_zero), tail_zero, ())
    key_piece = lax.all_gather(keys, "ctx", axis=0, tiled=True)
    value_piece = lax.all_gather(values, "ctx", axis=0, tiled=True)
    piece_rows = key_piece.shape[0]
    stride = math.gcd(piece_rows, local_rows)
    count = piece_rows // stride
    key_blocks = key_piece.reshape(count, stride, groups, HEAD_SIZE)
    value_blocks = value_piece.reshape(count, stride, groups, HEAD_SIZE)

    def fold_step(state, inputs):
        key_block, value_block, number = inputs
        first = number * stride
        key_pos = first + jnp.arange(stride, dtype=jnp.int32)
        parts_now, tails_now, states_now = state
        new_parts = (
            advance(parts_now[0], row_sets[0], key_block, value_block, key_pos, first),
            advance(parts_now[1], row_sets[1], key_block, value_block, key_pos, first),
        )
        earlier_block = first < own_start
        new_tails = lax.cond(
            earlier_block,
            lambda current: add_tail(current, key_block, value_block, key_pos),
            lambda current: current,
            tails_now,
        )
        return ((new_parts, new_tails, states_now), None)

    carry, unused = lax.scan(
        fold_step, carry, (key_blocks, value_blocks, jnp.arange(count, dtype=jnp.int32))
    )
    phi_own = features(proj_own)
    local_kv = split_product("grkf,kgd->grfd", phi_own, own_values)
    state_kv, state_norm = carried_in(
        (local_kv, jnp.sum(phi_own, axis=2)), "ctx", add_pair, state_zero
    )
    parts_done, tails_done = (carry[0], carry[1])
    teacher_first = parts_done[0][2] / parts_done[0][1][..., None]
    teacher_second = parts_done[1][2] / parts_done[1][1][..., None]
    teacher_second = return_partner(teacher_second)
    teacher = jnp.concatenate([teacher_first, teacher_second], axis=2)
    tail_key = tails_done[0].astype(jnp.bfloat16)
    tail_value = tails_done[1].astype(jnp.bfloat16)
    slab_key = jnp.concatenate([tail_key, own_keys], axis=0)
    slab_value = jnp.concatenate([tail_value, own_values], axis=0).astype(jnp.float32)
    slab_rows = WIN + local_rows
    slab_pos = own_start - WIN + jnp.arange(slab_rows, dtype=jnp.int32)
    is_tail = jnp.arange(slab_rows, dtype=jnp.int32) < WIN
    proj_tail = jnp.einsum("kgd,grdf->grkf", tail_key, weight4, preferred_element_type=jnp.float32)
    proj_slab = jnp.concatenate([proj_tail, proj_own], axis=2)
    phi_slab = features(proj_slab)
    proj_query = jnp.einsum("qgrd,grdf->grqf", query4, weight4, preferred_element_type=jnp.float32)
    phi_query = features(proj_query)
    scores = (
        jnp.einsum("qgrd,kgd->grqk", query4, slab_key, preferred_element_type=jnp.float32) * scale
    )
    window = (
        (slab_pos[None, :] >= query_pos[:, None] - WIN)
        & (slab_pos[None, :] <= query_pos[:, None])
        & (slab_pos[None, :] >= 0)
    )
    far = jnp.logical_not(is_tail)[None, :] & (slab_pos[None, :] < query_pos[:, None] - WIN)
    coefficient = far.astype(jnp.float32) - (window & is_tail[None, :]).astype(jnp.float32)
    window_top = jnp.max(jnp.where(window, scores, big_negative), axis=-1)
    local = jnp.exp(jnp.where(window, scores - window_top[..., None], big_negative))
    kernel = jnp.einsum("grqf,grkf->grqk", phi_query, phi_slab, precision=highest)
    mixed = local + coefficient * kernel
    numerator = jnp.einsum("grqk,kgd->grqd", mixed, slab_value, precision=highest) + jnp.einsum(
        "grqf,grfd->grqd", phi_query, state_kv, precision=highest
    )
    denominator = jnp.sum(mixed, axis=-1) + jnp.einsum(
        "grqf,grf->grq", phi_query, state_norm, precision=highest
    )
    student = numerator / denominator[..., None]
    error = student - teacher
    attn_error = jnp.transpose(error, (2, 0, 1, 3)).reshape(local_rows, heads_here * HEAD_SIZE)
    whole_rows = local_rows * ctx_count
    loss = lax.psum(jnp.sum(error * error), ("ctx", "head")) / (whole_rows * QUERY_HEADS)
    grad_out = 2.0 * error / denominator[..., None]
    grad_den = -jnp.sum(grad_out * student, axis=-1)
    later_kv = jnp.einsum("grqf,grqd->grfd", phi_query, grad_out, precision=highest)
    later_norm = jnp.einsum("grqf,grq->grf", phi_query, grad_den, precision=highest)
    suffix_kv, suffix_norm = prefix((later_kv, later_norm), "ctx", add_pair, state_zero)
    grad_lin = coefficient * (
        jnp.einsum("grqd,kgd->grqk", grad_out, slab_value, precision=highest) + grad_den[..., None]
    )
    grad_phi_query = (
        jnp.einsum("grqk,grkf->grqf", grad_lin, phi_slab, precision=highest)
        + jnp.einsum("grqd,grfd->grqf", grad_out, state_kv, precision=highest)
        + grad_den[..., None] * state_norm[:, :, None, :]
    )
    grad_phi_slab = jnp.einsum("grqk,grqf->grkf", grad_lin, phi_query, precision=highest)
    own_extra = (
        jnp.einsum("kgd,grfd->grkf", own_values.astype(jnp.float32), suffix_kv, precision=highest)
        + suffix_norm[:, :, None, :]
    )
    grad_phi_slab = grad_phi_slab + jnp.concatenate(
        [jnp.zeros((groups, group_ratio, WIN, 2 * FM), jnp.float32), own_extra], axis=2
    )
    grad_proj_query = feature_back(proj_query, grad_phi_query)
    grad_proj_slab = feature_back(proj_slab, grad_phi_slab)
    grad_local = jnp.einsum(
        "qgrd,grqf->grdf", query4.astype(jnp.float32), grad_proj_query, precision=highest
    ) + jnp.einsum(
        "kgd,grkf->grdf", slab_key.astype(jnp.float32), grad_proj_slab, precision=highest
    )
    grad_w = lax.psum(grad_local.reshape(heads_here, HEAD_SIZE, FM), "ctx")
    return (attn_error, loss, grad_w)


def solution(mesh):
    placed = (P("ctx", "head"), P("ctx", "head"), P("ctx", "head"), P("head", None, None))
    return jax.shard_map(
        shards,
        mesh=mesh,
        in_specs=placed,
        out_specs=(P("ctx", "head"), P(), P("head", None, None)),
        check_vma=False,
    )
```

profile of v0, /device:TPU:0, one launch (start us, length us, event | category | flops | bytes accessed | tf_op | source)
XLA Modules:
  0.0 783.3 jit_solution(9861084651910707477)
XLA Ops:
  25.6 4.3 fusion.116
  29.9 8.6 %collective-permute-done.1 = bf16[64,4,8,128]{3,2,1,0:T(8,128)(2,1)} collective-permute-done((bf16[64,4,8,128]{3,2,1,0:T(8,128)(2,1)}, bf16[64,4,8,128]{3,2,1,0:T(8,128)(2,1)}, u32[]{:S(2)}, u32[]{:S(2)}) %collective-permute-start.1) | collective-permute-done | bytes 524320 | tf_op jit(solution)/shard_map/ppermute | solution.py:20
  40.3 5.5 fusion.79
  45.8 13.8 %collective-permute-done.2 = bf16[64,4,8,128]{3,2,1,0:T(8,128)(2,1)} collective-permute-done((bf16[64,4,8,128]{3,2,1,0:T(8,128)(2,1)}, bf16[64,4,8,128]{3,2,1,0:T(8,128)(2,1)}, u32[]{:S(2)}, u32[]{:S(2)}) %collective-permute-start.2) | collective-permute-done | bytes 524320 | tf_op jit(solution)/shard_map/ppermute | solution.py:20
  64.5 4.3 maximum_multiply_fusion.1
  68.9 20.4 %collective-permute-done.3 = bf16[64,4,8,128]{3,2,1,0:T(8,128)(2,1)} collective-permute-done((bf16[64,4,8,128]{3,2,1,0:T(8,128)(2,1)}, bf16[64,4,8,128]{3,2,1,0:T(8,128)(2,1)}, u32[]{:S(2)}, u32[]{:S(2)}) %collective-permute-start.3) | collective-permute-done | bytes 524320 | tf_op jit(solution)/shard_map/ppermute | solution.py:20
  91.4 4.4 reshape.276
  95.8 16.4 %all-gather.11.cloned.1.call-done = bf16[2048,512]{1,0:T(8,128)(2,1)} async-done(((bf16[128,512]{1,0:T(8,128)(2,1)}), bf16[2048,512]{1,0:T(8,128)(2,1)}) %all-gather.11.cloned.1.call-update) | async-done | bytes 2097168 | tf_op jit(solution)/shard_map/all_gather | solution.py:198
  112.2 4.0 reshape.277
  118.3 193.6 %while.59 = (s32[]{:T(128)}, f32[4,8,64]{2,1,0:T(8,128)S(1)}, f32[4,8,64]{2,1,0:T(8,128)S(1)}, f32[4,8,64,128]{3,2,1,0:T(8,128)S(1)}, f32[4,8,64]{2,1,0:T(8,128)...) while((s32[]{:T(128)}, f32[4,8,64]{2,1,0:T(8,128)S(1)}, ...), condition=%wide.region_17.18_spmd.clone, body=%wide.region_0.17_spmd.clone.sunk | while | flops 291086528 | bytes 14226523 | solution.py:223
  316.5 64.0 %all-gather.1 = bf16[64,8,128]{2,1,0:T(8,128)(2,1)} all-gather(bf16[4,8,128]{2,1,0:T(8,128)(2,1)S(1)} %fusion.143), channel_id=3, replica_groups=mesh['ctx'=16,'head'=2] {'ctx'}, dimensions={0}, use_global_device_ids=true | all-gather | bytes 139264 | tf_op jit(solution)/shard_map/all_gather | solution.py:26
  384.5 4.6 fusion.46
  389.1 4.7 fusion.109
  393.8 4.8 collective-permute-done.5
  400.9 11.1 %collective-permute-done.6 = bf16[4,8,64,128]{3,2,1,0:T(8,128)(2,1)S(1)} collective-permute-done((bf16[4,8,64,128]{3,2,1,0:T(8,128)(2,1)S(1)}, bf16[4,8,64,128]{3,2,1,0:T(8,128)(2,1)S(1)}, u32[]{:S(2)}, u32[]{:S(2)}) %collective-permute-start.6) | collective-permute-done | bytes 524320 | tf_op jit(solution)/shard_map/ppermute | solution.py:20
  413.3 5.2 fusion.122
  418.5 18.1 %collective-permute-done.7 = bf16[4,8,64,128]{3,2,1,0:T(8,128)(2,1)S(1)} collective-permute-done((bf16[4,8,64,128]{3,2,1,0:T(8,128)(2,1)S(1)}, bf16[4,8,64,128]{3,2,1,0:T(8,128)(2,1)S(1)}, u32[]{:S(2)}, u32[]{:S(2)}) %collective-permute-start.7) | collective-permute-done | bytes 524320 | tf_op jit(solution)/shard_map/ppermute | solution.py:20
  437.7 49.1 %while.60 = (s32[]{:T(128)}, f32[4,8,128,128]{3,2,1,0:T(8,128)S(1)}, f32[4,8,128]{2,1,0:T(8,128)S(1)}, s32[]{:T(128)}, bf16[16,4,8,128,128]{4,3,2,1,0:T(8,128)(2...) while((s32[]{:T(128)}, f32[4,8,128,128]{3,2,1,0:T(8,128)S(1)}, ...), condition=%wide.region_21.22_spmd.clone, body=%wide.region_20.21_spmd.clone.sunk | while | flops 2113540 | bytes 5283955 | solution.py:43
  486.7 5.7 fusion.150
  492.5 6.4 multiply_reduce_fusion
  500.2 4.6 convolution_convert_fusion
  505.4 3.6 fusion.151
  509.0 19.1 %all-gather.3 = bf16[64,8,128]{2,1,0:T(8,128)(2,1)S(1)} all-gather(bf16[4,8,128]{2,1,0:T(8,128)(2,1)S(1)} %convert_element_type.142), channel_id=5, replica_groups=mesh['ctx'=16,'head'=2] {'ctx'}, dimensions={0}, use_global_device_ids=true | all-gather | bytes 139264 | tf_op jit(solution)/shard_map/all_gather | solution.py:49
  531.3 7.9 %fusion.68 = f32[4,8,128,128]{3,2,1,0:T(8,128)S(1)} fusion(f32[4,8,128,192]{2,3,1,0:T(8,128)S(1)} %fusion.121, f32[4,8,128]{2,1,0:T(8,128)S(1)} %neg.21, f32[128,192]{0,1:T(8,128)S(1)} %convert_subtract_fusion, f32[4,8,192,64]{3,2,1,0:T(8,128)S(1)} %copy-done.11, f32[4,8,192,64]{3,2,1,0:T(8,128)S(1)} %copy-done.9), kind=kOutput, calls=%fused_computation.116 | convolution fusion | flops 1211105280 | bytes 8503296 | tf_op jit(solution)/shard_map/grqk,grkf->grqf/dot_general | solution.py:282
  539.2 4.8 multiply_add_fusion.4
  544.1 4.5 fusion.83
  548.6 81.4 %all-gather.15.cloned.1.call-done = bf16[64,8,128,128]{3,2,1,0:T(8,128)(2,1)} async-done(((bf16[4,8,128,128]{3,2,1,0:T(8,128)(2,1)}), bf16[64,8,128,128]{3,2,1,0:T(8,128)(2,1)}) %all-gather.15.cloned.1.call-update) | async-done | bytes 16777232 | tf_op jit(solution)/shard_map/all_gather | solution.py:49
  630.0 38.6 %while.61 = (s32[]{:T(128)}, f32[4,8,128,128]{3,2,1,0:T(8,128)S(1)}, f32[4,8,128]{2,1,0:T(8,128)S(1)}, s32[]{:T(128)}, bf16[16,4,8,128,128]{4,3,2,1,0:T(8,128)(2...) while((s32[]{:T(128)}, ...), condition=%wide.region_27.28_spmd.clone, body=%wide.region_26.27_spmd.clone.sunk | while | flops 2113544 | bytes 5284017 | solution.py:67
  670.2 5.7 pad_add_fusion
  675.9 5.3 fusion.102
  681.2 39.0 %psum.14 = f32[]{:T(128)} all-reduce(f32[]{:T(128)} %get-tuple-element.673), channel_id=1, replica_groups=mesh['ctx'=16,'head'=2] {'ctx','head'}, use_global_device_ids=true, to_apply=%region_24.25 | all-reduce | flops 1 | bytes 8 | tf_op jit(solution)/shard_map/psum | solution.py:272
  724.6 48.3 %all-reduce.3.cloned.1.call-done = f32[32,128,64]{1,2,0:T(8,128)} async-done(((f32[32,128,64]{1,2,0:T(8,128)}), f32[32,128,64]{1,2,0:T(8,128)}) %all-reduce.3.cloned.1.call-update) | async-done | bytes 1048592 | tf_op jit(solution)/shard_map/psum | solution.py:301
  (483 shorter events, 321.2 us)
Async XLA Ops:
  7.2 84.2 %all-gather.9.cloned.1.call-start = ((), (), s32[]{:S(2)}) async-start(), calls=%async_computation | async-start | bytes 2228224 | tf_op jit(solution)/shard_map/all_gather | solution.py:197
  7.9 104.2 %all-gather.11.cloned.1.call-start = ((), (), s32[]{:S(2)}) async-start(), calls=%async_computation.1 | async-start | bytes 2228224 | tf_op jit(solution)/shard_map/all_gather | solution.py:198
  8.7 429.0 %all-gather.13.cloned.1.call-start = ((), (), s32[]{:S(2)}) async-start(), calls=%async_computation.3 | async-start | bytes 17825792 | tf_op jit(solution)/shard_map/all_gather | solution.py:26
  10.8 53.0 %copy-start.22 = (bf16[128,512]{0,1:T(8,128)(2,1)}, bf16[128,512]{0,1:T(8,128)(2,1)S(1)}, u32[]{:S(2)}) copy-start(bf16[128,512]{0,1:T(8,128)(2,1)S(1)} %copy.138) | copy-start | bytes 393220
  17.9 612.1 %all-gather.15.cloned.1.call-start = ((), (), s32[]{:S(2)}) async-start(), calls=%async_computation.4 | async-start | bytes 17825792 | tf_op jit(solution)/shard_map/all_gather | solution.py:49
  20.1 2.9 collective-permute-start
  23.1 15.4 %collective-permute-start.1 = (bf16[64,4,8,128]{3,2,1,0:T(8,128)(2,1)}, bf16[64,4,8,128]{3,2,1,0:T(8,128)(2,1)}, u32[]{:S(2)}, u32[]{:S(2)}) collective-permute-start(bf16[64,4,8,128]{3,2,1,0:T(8,128)(2,1)} %collective-permute-done), channel_id=1, source_target_pairs={{0,4},{2,6},{4,0},{6,2},{8,12},{10,14},{12,8},{14,10},{16,20},{18,... | collective-permute-start | bytes 1572872 | tf_op jit(solution)/shard_map/ppermute | solution.py:20
  29.9 16.0 %copy-start.28 = (u8[4,128,64]{2,1,0:T(8,128)(4,1)}, u8[4,128,64]{2,1,0:T(8,128)(4,1)S(1)}, u32[]{:S(2)}) copy-start(u8[4,128,64]{2,1,0:T(8,128)(4,1)S(1)} %get-tuple-element.671) | copy-start | bytes 98308
  38.5 21.1 %collective-permute-start.2 = (bf16[64,4,8,128]{3,2,1,0:T(8,128)(2,1)}, bf16[64,4,8,128]{3,2,1,0:T(8,128)(2,1)}, u32[]{:S(2)}, u32[]{:S(2)}) collective-permute-start(bf16[64,4,8,128]{3,2,1,0:T(8,128)(2,1)} %collective-permute-done.1), channel_id=1, source_target_pairs={{0,8},{2,10},{4,12},{6,14},{8,0},{10,2},{12,4},{14,6},{16,24},{18,... | collective-permute-start | bytes 1572872 | tf_op jit(solution)/shard_map/ppermute | solution.py:20
  40.3 21.7 %copy-start.14 = (f32[4,8,128,64]{3,2,1,0:T(8,128)S(1)}, f32[4,8,128,64]{3,2,1,0:T(8,128)}, u32[]{:S(2)}) copy-start(f32[4,8,128,64]{3,2,1,0:T(8,128)} %copy-done.13) | copy-start | bytes 3145732
  59.6 29.8 %collective-permute-start.3 = (bf16[64,4,8,128]{3,2,1,0:T(8,128)(2,1)}, bf16[64,4,8,128]{3,2,1,0:T(8,128)(2,1)}, u32[]{:S(2)}, u32[]{:S(2)}) collective-permute-start(bf16[64,4,8,128]{3,2,1,0:T(8,128)(2,1)} %collective-permute-done.2), channel_id=1, source_target_pairs={{0,16},{2,18},{4,20},{6,22},{8,24},{10,26},{12,28},{14,30},{16,0},... | collective-permute-start | bytes 1572872 | tf_op jit(solution)/shard_map/ppermute | solution.py:20
  313.0 71.4 %collective-permute-start.4 = (bf16[4,8,64,128]{3,2,1,0:T(8,128)(2,1)}, bf16[4,8,64,128]{3,2,1,0:T(8,128)(2,1)S(1)}, u32[]{:S(2)}, u32[]{:S(2)}) collective-permute-start(bf16[4,8,64,128]{3,2,1,0:T(8,128)(2,1)} %divide_convert_fusion), channel_id=1, source_target_pairs={{0,2},{2,0},{4,6},{6,4},{8,10},{10,8},{12,14},{14,12},{16,18},{18,... | collective-permute-start | bytes 1572872 | tf_op jit(solution)/shard_map/ppermute | solution.py:20
  384.4 14.2 %collective-permute-start.5 = (bf16[4,8,64,128]{3,2,1,0:T(8,128)(2,1)S(1)}, bf16[4,8,64,128]{3,2,1,0:T(8,128)(2,1)S(1)}, u32[]{:S(2)}, u32[]{:S(2)}) collective-permute-start(bf16[4,8,64,128]{3,2,1,0:T(8,128)(2,1)S(1)} %collective-permute-done.4), channel_id=1, source_target_pairs={{0,4},{2,6},{4,0},{6,2},{8,12},{10,14},{12,8},{14,10},{16,20},{18,... | collective-permute-start | bytes 1572872 | tf_op jit(solution)/shard_map/ppermute | solution.py:20
  389.1 9.6 %copy-start.20 = (bf16[16,8,32,128]{3,2,1,0:T(8,128)(2,1)S(1)}, bf16[16,8,32,128]{3,2,1,0:T(8,128)(2,1)}, u32[]{:S(2)}) copy-start(bf16[16,8,32,128]{3,2,1,0:T(8,128)(2,1)} %copy.204) | copy-start | bytes 3145732
  389.1 9.6 %copy-start.27 = (bf16[128,4,128]{2,0,1:T(8,128)(2,1)S(1)}, bf16[128,4,128]{2,0,1:T(8,128)(2,1)}, u32[]{:S(2)}) copy-start(bf16[128,4,128]{2,0,1:T(8,128)(2,1)} %copy.128) | copy-start | bytes 393220
  393.8 5.5 copy-start.17
  398.6 13.4 %collective-permute-start.6 = (bf16[4,8,64,128]{3,2,1,0:T(8,128)(2,1)S(1)}, bf16[4,8,64,128]{3,2,1,0:T(8,128)(2,1)S(1)}, u32[]{:S(2)}, u32[]{:S(2)}) collective-permute-start(bf16[4,8,64,128]{3,2,1,0:T(8,128)(2,1)S(1)} %collective-permute-done.5), channel_id=1, source_target_pairs={{0,8},{2,10},{4,12},{6,14},{8,0},{10,2},{12,4},{14,6},{16,24},{18,... | collective-permute-start | bytes 1572872 | tf_op jit(solution)/shard_map/ppermute | solution.py:20
  400.9 12.4 %copy-start.26 = (bf16[128,4,128]{2,0,1:T(8,128)(2,1)S(1)}, bf16[128,4,128]{2,0,1:T(8,128)(2,1)}, u32[]{:S(2)}) copy-start(bf16[128,4,128]{2,0,1:T(8,128)(2,1)} %copy.139) | copy-start | bytes 393220
  412.0 24.6 %collective-permute-start.7 = (bf16[4,8,64,128]{3,2,1,0:T(8,128)(2,1)S(1)}, bf16[4,8,64,128]{3,2,1,0:T(8,128)(2,1)S(1)}, u32[]{:S(2)}, u32[]{:S(2)}) collective-permute-start(bf16[4,8,64,128]{3,2,1,0:T(8,128)(2,1)S(1)} %collective-permute-done.6), channel_id=1, source_target_pairs={{0,16},{2,18},{4,20},{6,22},{8,24},{10,26},{12,28},{14,30},{16,0},... | collective-permute-start | bytes 1572872 | tf_op jit(solution)/shard_map/ppermute | solution.py:20
  413.3 24.3 %copy-start.2 = (f32[4,8,128,128]{3,2,1,0:T(8,128)S(1)}, f32[4,8,128,128]{3,2,1,0:T(8,128)}, u32[]{:S(2)}) copy-start(f32[4,8,128,128]{3,2,1,0:T(8,128)} %custom-call) | copy-start | bytes 6291460
  486.7 12.1 %copy-start.3 = (f32[4,8,128,128]{3,2,1,0:T(8,128)}, f32[4,8,128,128]{3,2,1,0:T(8,128)S(1)}, u32[]{:S(2)}) copy-start(f32[4,8,128,128]{3,2,1,0:T(8,128)S(1)} %get-tuple-element.496) | copy-start | bytes 6291460
  486.7 5.8 copy-start.6
  504.8 268.1 %all-reduce.3.cloned.1.call-start = ((), (), s32[]{:S(2)}) async-start(), calls=%async_computation.2 | async-start | bytes 2097152 | tf_op jit(solution)/shard_map/psum | solution.py:301
  505.3 25.9 %copy-start.11 = (f32[4,8,192,64]{3,2,1,0:T(8,128)S(1)}, f32[4,8,192,64]{3,2,1,0:T(8,128)}, u32[]{:S(2)}) copy-start(f32[4,8,192,64]{3,2,1,0:T(8,128)} %copy-done.10) | copy-start | bytes 4718596
  531.3 7.9 %copy-start.12 = (f32[4,8,128,192]{2,3,1,0:T(8,128)}, f32[4,8,128,192]{2,3,1,0:T(8,128)S(1)}, u32[]{:S(2)}) copy-start(f32[4,8,128,192]{2,3,1,0:T(8,128)S(1)} %fusion.121) | copy-start | bytes 9437188
  531.3 7.9 %copy-start.4 = (f32[4,8,128,128]{3,2,1,0:T(8,128)S(1)}, f32[4,8,128,128]{3,2,1,0:T(8,128)}, u32[]{:S(2)}) copy-start(f32[4,8,128,128]{3,2,1,0:T(8,128)} %copy-done.3) | copy-start | bytes 6291460
  531.3 7.9 %copy-start.16 = (f32[4,8,128,128]{3,2,1,0:T(8,128)S(1)}, f32[4,8,128,128]{3,2,1,0:T(8,128)}, u32[]{:S(2)}) copy-start(f32[4,8,128,128]{3,2,1,0:T(8,128)} %copy-done.15) | copy-start | bytes 6291460
  630.0 38.6 %copy-start.23 = (bf16[128,512]{0,1:T(8,128)(2,1)S(1)}, bf16[128,512]{0,1:T(8,128)(2,1)}, u32[]{:S(2)}) copy-start(bf16[128,512]{0,1:T(8,128)(2,1)} %copy-done.22) | copy-start | bytes 393220
  670.2 5.7 copy-start.19
  670.2 5.8 copy-start.25
  670.2 5.8 copy-start.31
  722.1 53.1 %copy-start.1 = (bf16[32,128,64]{1,2,0:T(8,128)(2,1)S(1)}, bf16[32,128,64]{1,2,0:T(8,128)(2,1)}, u32[]{:S(2)}) copy-start(bf16[32,128,64]{1,2,0:T(8,128)(2,1)} %param.21) | copy-start | bytes 1572868
  (13 other events, 49.1 us)
Sparse Core Ops, SparseCore 0:
  10.2 45.6 all-gather.8
  58.0 54.1 all-gather.10
  114.3 125.7 all-gather.12
  505.0 124.9 all-gather.14
  681.3 91.5 all-reduce.2
where the time goes:
time: 796 us; the launch traced here: 783 us
  waiting for transfers between devices  224 us (28%)
  blocking collectives  122 us (15%)
  matrix products  120 us (15%)
  other arithmetic  120 us (15%)
  local copies, waits for them, and re-layouts  96.2 us (12%)
  loops' own time  72.7 us (9%)
  between operations  16.5 us (2%)
  starting transfers between devices  11 us (1%)
    all_gather x1, waiting for transfers between devices, prefix(): lax.all_gather(part.astype(kind), axis)  81.4 us
    ppermute x8, waiting for transfers between devices, swapped(): return lax.ppermute(value, axis, pairs)  76.8 us
    another operation x1, loops' own time, shards(): lax.scan(fold_step, carry, (key_blocks, value_blocks, jnp.arange(count, d...  70.5 us
    all_gather x1, blocking collectives, carried_in(): lax.all_gather(part.astype(kind), axis)  64 us
    select_n x32, other arithmetic, carried_step(): return jax.tree.map(lambda a, b: jnp.where(reached, a, b), new, before)  49 us
    psum x1, waiting for transfers between devices, shards(): grad_w = lax.psum(grad_local.reshape(heads_here, HEAD_SIZE, FM), 'ctx')  48.3 us
    psum x1, blocking collectives, shards(): lax.psum(jnp.sum(error * error), ('ctx', 'head'))  39 us
    dynamic_slice x64, local copies, waits for them, and re-layouts, shards(): lax.scan(fold_step, carry, (key_blocks, value_blocks, jnp.arange(count, d...  38.7 us
  transfers between devices with their start and end apart: 13, of which 9 were waited for; matrix products, arithmetic and copies ran while one was open for 28% of the time, Pallas kernels for 0%

commit v1 on v0

--- a/solution.py
+++ b/solution.py
@@ -195,7 +195,16 @@
     )
     carry = ((part_zero, part_zero), tail_zero, ())
     key_piece = lax.all_gather(keys, "ctx", axis=0, tiled=True)
-    value_piece = lax.all_gather(values, "ctx", axis=0, tiled=True)
+    block_out, h_now = (lax.psum(1, "ctx"), lax.axis_index("ctx"))
+    value_piece, formed = (values, 1)
+    while formed < block_out:
+        outcome_arr = lax.ppermute(
+            value_piece, "ctx", [(dd, dd ^ formed) for dd in range(block_out)]
+        )
+        vec_out = jnp.concatenate([value_piece, outcome_arr], axis=0)
+        piece_next = jnp.concatenate([outcome_arr, value_piece], axis=0)
+        value_piece = jnp.where(h_now & formed == 0, vec_out, piece_next)
+        formed = 2 * formed
     piece_rows = key_piece.shape[0]
     stride = math.gcd(piece_rows, local_rows)
     count = piece_rows // stride

time: 796 us -> 840 us (1.055)
  waiting for transfers between devices: 224 us -> 263 us
    ppermute x0 -> x4, waiting for transfers between devices: none -> 57.4 us  [shards(): lax.ppermute(value_piece, 'ctx', [(dd, dd ^ formed) for dd in range(block...]
    all_gather x1 -> x0, waiting for transfers between devices: 16.4 us -> none  [shards(): value_piece = lax.all_gather(values, 'ctx', axis=0, tiled=True)]
    ppermute x0 -> x4, starting transfers between devices: none -> 8.61 us  [shards(): lax.ppermute(value_piece, 'ctx', [(dd, dd ^ formed) for dd in range(block...]
  transfers between devices with their start and end apart: 13 -> 16, of which waited for: 9 -> 12; matrix products, arithmetic and copies ran while one was open for 28% -> 26% of each run, Pallas kernels for 0% -> 0%
where the time goes in v1:
time: 840 us; the launch traced here: 831 us
  waiting for transfers between devices  263 us (31%)
  other arithmetic  124 us (15%)
  blocking collectives  122 us (15%)
  matrix products  119 us (14%)
  local copies, waits for them, and re-layouts  96.8 us (12%)
  loops' own time  71.7 us (9%)
  starting transfers between devices  17.9 us (2%)
  between operations  16.4 us (2%)
    all_gather x1, waiting for transfers between devices, prefix(): lax.all_gather(part.astype(kind), axis)  81.1 us
    ppermute x8, waiting for transfers between devices, swapped(): return lax.ppermute(value, axis, pairs)  75.5 us
    another operation x1, loops' own time, shards(): lax.scan(fold_step, carry, (key_blocks, value_blocks, jnp.arange(count, d...  69.6 us
    all_gather x1, blocking collectives, carried_in(): lax.all_gather(part.astype(kind), axis)  63.9 us
    ppermute x4, waiting for transfers between devices, shards(): lax.ppermute(value_piece, 'ctx', [(dd, dd ^ formed) for dd in range(block...  57.4 us
    select_n x32, other arithmetic, carried_step(): return jax.tree.map(lambda a, b: jnp.where(reached, a, b), new, before)  49 us
    psum x1, waiting for transfers between devices, shards(): grad_w = lax.psum(grad_local.reshape(heads_here, HEAD_SIZE, FM), 'ctx')  48.3 us
    psum x1, blocking collectives, shards(): lax.psum(jnp.sum(error * error), ('ctx', 'head'))  38.9 us
  transfers between devices with their start and end apart: 16, of which 12 were waited for; matrix products, arithmetic and copies ran while one was open for 26% of the time, Pallas kernels for 0%

profile of v1, /device:TPU:0, one launch (start us, length us, event | category | flops | bytes accessed | tf_op | source)
XLA Modules:
  0.0 831.1 jit_solution(527087233811665068)
XLA Ops:
  26.6 3.7 collective-permute-done.1
  37.6 12.2 %collective-permute-done.2 = bf16[512,512]{1,0:T(8,128)(2,1)} collective-permute-done((bf16[512,512]{1,0:T(8,128)(2,1)S(1)}, bf16[512,512]{1,0:T(8,128)(2,1)}, u32[]{:S(2)}, u32[]{:S(2)}) %collective-permute-start.2) | collective-permute-done | bytes 524320 | tf_op jit(solution)/shard_map/ppermute | solution.py:201
  61.1 28.5 %collective-permute-done.6 = bf16[64,4,8,128]{3,2,1,0:T(8,128)(2,1)} collective-permute-done((bf16[64,4,8,128]{3,2,1,0:T(8,128)(2,1)}, bf16[64,4,8,128]{3,2,1,0:T(8,128)(2,1)}, u32[]{:S(2)}, u32[]{:S(2)}) %collective-permute-start.6) | collective-permute-done | bytes 524320 | tf_op jit(solution)/shard_map/ppermute | solution.py:20
  89.6 4.4 collective-permute-start.7
  97.3 40.5 %collective-permute-done.3 = bf16[1024,512]{1,0:T(8,128)(2,1)} collective-permute-done((bf16[1024,512]{1,0:T(8,128)(2,1)}, bf16[1024,512]{1,0:T(8,128)(2,1)}, u32[]{:S(2)}, u32[]{:S(2)}) %collective-permute-start.3) | collective-permute-done | bytes 1048608 | tf_op jit(solution)/shard_map/ppermute | solution.py:201
  137.9 4.3 maximum_select_fusion
  142.1 4.4 reshape.278
  146.6 12.9 %collective-permute-done.7 = bf16[64,4,8,128]{3,2,1,0:T(8,128)(2,1)} collective-permute-done((bf16[64,4,8,128]{3,2,1,0:T(8,128)(2,1)}, bf16[64,4,8,128]{3,2,1,0:T(8,128)(2,1)}, u32[]{:S(2)}, u32[]{:S(2)}) %collective-permute-start.7) | collective-permute-done | bytes 524320 | tf_op jit(solution)/shard_map/ppermute | solution.py:20
  161.6 4.1 reshape.277
  167.9 192.6 %while.59 = (s32[]{:T(128)}, f32[4,8,64]{2,1,0:T(8,128)S(1)}, f32[4,8,64]{2,1,0:T(8,128)S(1)}, f32[4,8,64,128]{3,2,1,0:T(8,128)S(1)}, f32[4,8,64]{2,1,0:T(8,128)...) while((s32[]{:T(128)}, f32[4,8,64]{2,1,0:T(8,128)S(1)}, ...), condition=%wide.region_17.18_spmd.clone, body=%wide.region_0.17_spmd.clone.sunk | while | flops 291086528 | bytes 14226523 | solution.py:232
  364.0 63.9 %all-gather.1 = bf16[64,8,128]{2,1,0:T(8,128)(2,1)} all-gather(bf16[4,8,128]{2,1,0:T(8,128)(2,1)S(1)} %fusion.143), channel_id=3, replica_groups=mesh['ctx'=16,'head'=2] {'ctx'}, dimensions={0}, use_global_device_ids=true | all-gather | bytes 139264 | tf_op jit(solution)/shard_map/all_gather | solution.py:26
  432.6 4.6 fusion.46
  437.2 4.7 fusion.109
  441.9 4.8 collective-permute-done.9
  449.0 11.1 %collective-permute-done.10 = bf16[4,8,64,128]{3,2,1,0:T(8,128)(2,1)S(1)} collective-permute-done((bf16[4,8,64,128]{3,2,1,0:T(8,128)(2,1)S(1)}, bf16[4,8,64,128]{3,2,1,0:T(8,128)(2,1)S(1)}, u32[]{:S(2)}, u32[]{:S(2)}) %collective-permute-start.10) | collective-permute-done | bytes 524320 | tf_op jit(solution)/shard_map/ppermute | solution.py:20
  461.4 5.2 fusion.122
  466.6 18.0 %collective-permute-done.11 = bf16[4,8,64,128]{3,2,1,0:T(8,128)(2,1)S(1)} collective-permute-done((bf16[4,8,64,128]{3,2,1,0:T(8,128)(2,1)S(1)}, bf16[4,8,64,128]{3,2,1,0:T(8,128)(2,1)S(1)}, u32[]{:S(2)}, u32[]{:S(2)}) %collective-permute-start.11) | collective-permute-done | bytes 524320 | tf_op jit(solution)/shard_map/ppermute | solution.py:20
  485.8 49.1 %while.60 = (s32[]{:T(128)}, f32[4,8,128,128]{3,2,1,0:T(8,128)S(1)}, f32[4,8,128]{2,1,0:T(8,128)S(1)}, s32[]{:T(128)}, bf16[16,4,8,128,128]{4,3,2,1,0:T(8,128)(2...) while((s32[]{:T(128)}, f32[4,8,128,128]{3,2,1,0:T(8,128)S(1)}, ...), condition=%wide.region_21.22_spmd.clone, body=%wide.region_20.21_spmd.clone.sunk | while | flops 2113540 | bytes 5283955 | solution.py:43
  534.8 5.7 fusion.150
  540.6 6.4 multiply_reduce_fusion
  548.3 4.6 convolution_convert_fusion
  553.5 3.6 fusion.151
  557.1 19.3 %all-gather.3 = bf16[64,8,128]{2,1,0:T(8,128)(2,1)S(1)} all-gather(bf16[4,8,128]{2,1,0:T(8,128)(2,1)S(1)} %convert_element_type.142), channel_id=5, replica_groups=mesh['ctx'=16,'head'=2] {'ctx'}, dimensions={0}, use_global_device_ids=true | all-gather | bytes 139264 | tf_op jit(solution)/shard_map/all_gather | solution.py:49
  579.7 7.9 fusion.68
  587.6 4.8 multiply_add_fusion.4
  592.4 4.5 fusion.83
  596.9 81.1 %all-gather.12.cloned.1.call-done = bf16[64,8,128,128]{3,2,1,0:T(8,128)(2,1)} async-done(((bf16[4,8,128,128]{3,2,1,0:T(8,128)(2,1)}), bf16[64,8,128,128]{3,2,1,0:T(8,128)(2,1)}) %all-gather.12.cloned.1.call-update) | async-done | bytes 16777232 | tf_op jit(solution)/shard_map/all_gather | solution.py:49
  678.0 38.6 %while.61 = (s32[]{:T(128)}, f32[4,8,128,128]{3,2,1,0:T(8,128)S(1)}, f32[4,8,128]{2,1,0:T(8,128)S(1)}, s32[]{:T(128)}, bf16[16,4,8,128,128]{4,3,2,1,0:T(8,128)(2...) while((s32[]{:T(128)}, ...), condition=%wide.region_27.28_spmd.clone, body=%wide.region_26.27_spmd.clone.sunk | while | flops 2113544 | bytes 5284017 | solution.py:67
  718.2 5.7 pad_add_fusion
  724.0 5.3 fusion.102
  729.3 38.9 %psum.14 = f32[]{:T(128)} all-reduce(f32[]{:T(128)} %get-tuple-element.673), channel_id=1, replica_groups=mesh['ctx'=16,'head'=2] {'ctx','head'}, use_global_device_ids=true, to_apply=%region_24.25 | all-reduce | flops 1 | bytes 8 | tf_op jit(solution)/shard_map/psum | solution.py:281
  772.6 48.3 %all-reduce.3.cloned.1.call-done = f32[32,128,64]{1,2,0:T(8,128)} async-done(((f32[32,128,64]{1,2,0:T(8,128)}), f32[32,128,64]{1,2,0:T(8,128)}) %all-reduce.3.cloned.1.call-update) | async-done | bytes 1048592 | tf_op jit(solution)/shard_map/psum | solution.py:310
  (504 shorter events, 336.7 us)
Async XLA Ops:
  7.2 154.4 %all-gather.8.cloned.1.call-start = ((), (), s32[]{:S(2)}) async-start(), calls=%async_computation | async-start | bytes 2228224 | tf_op jit(solution)/shard_map/all_gather | solution.py:197
  7.9 477.8 %all-gather.10.cloned.1.call-start = ((), (), s32[]{:S(2)}) async-start(), calls=%async_computation.2 | async-start | bytes 17825792 | tf_op jit(solution)/shard_map/all_gather | solution.py:26
  10.1 86.4 %copy-start.23 = (bf16[128,512]{0,1:T(8,128)(2,1)}, bf16[128,512]{0,1:T(8,128)(2,1)S(1)}, u32[]{:S(2)}) copy-start(bf16[128,512]{0,1:T(8,128)(2,1)S(1)} %copy.138) | copy-start | bytes 393220
  17.2 660.8 %all-gather.12.cloned.1.call-start = ((), (), s32[]{:S(2)}) async-start(), calls=%async_computation.3 | async-start | bytes 17825792 | tf_op jit(solution)/shard_map/all_gather | solution.py:49
  17.6 1.5 collective-permute-start
  19.2 11.1 %collective-permute-start.1 = (bf16[256,512]{1,0:T(8,128)(2,1)S(1)}, bf16[256,512]{1,0:T(8,128)(2,1)}, u32[]{:S(2)}, u32[]{:S(2)}) collective-permute-start(bf16[256,512]{1,0:T(8,128)(2,1)S(1)} %maximum_select_fusion.3), channel_id=1, source_target_pairs={{0,4},{2,6},{4,0},{6,2},{8,12},{10,14},{12,8},{14,10},{16,20},{18,... | collective-permute-start | bytes 786440 | tf_op jit(solution)/shard_map/ppermute | solution.py:201
  25.1 11.3 %collective-permute-start.4 = (bf16[64,4,8,128]{3,2,1,0:T(8,128)(2,1)}, bf16[64,4,8,128]{3,2,1,0:T(8,128)(2,1)}, u32[]{:S(2)}, u32[]{:S(2)}) collective-permute-start(bf16[64,4,8,128]{3,2,1,0:T(8,128)(2,1)} %bitcast.96), channel_id=1, source_target_pairs={{0,2},{2,0},{4,6},{6,4},{8,10},{10,8},{12,14},{14,12},{16,18},{18,... | collective-permute-start | bytes 1572872 | tf_op jit(solution)/shard_map/ppermute | solution.py:20
  26.5 9.9 %copy-start.20 = (bf16[16,8,32,128]{3,2,1,0:T(8,128)(2,1)}, bf16[16,8,32,128]{3,2,1,0:T(8,128)(2,1)S(1)}, u32[]{:S(2)}) copy-start(bf16[16,8,32,128]{3,2,1,0:T(8,128)(2,1)S(1)} %copy.204) | copy-start | bytes 3145732
  31.4 18.4 %collective-permute-start.2 = (bf16[512,512]{1,0:T(8,128)(2,1)S(1)}, bf16[512,512]{1,0:T(8,128)(2,1)}, u32[]{:S(2)}, u32[]{:S(2)}) collective-permute-start(bf16[512,512]{1,0:T(8,128)(2,1)S(1)} %maximum_select_fusion.2), channel_id=1, source_target_pairs={{0,8},{2,10},{4,12},{6,14},{8,0},{10,2},{12,4},{14,6},{16,24},{18,... | collective-permute-start | bytes 1572872 | tf_op jit(solution)/shard_map/ppermute | solution.py:201
  36.4 22.7 %copy-start.34 = (u8[4,128,64]{2,1,0:T(8,128)(4,1)}, u8[4,128,64]{2,1,0:T(8,128)(4,1)S(1)}, u32[]{:S(2)}) copy-start(u8[4,128,64]{2,1,0:T(8,128)(4,1)S(1)} %get-tuple-element.671) | copy-start | bytes 98308
  36.4 19.5 %collective-permute-start.5 = (bf16[64,4,8,128]{3,2,1,0:T(8,128)(2,1)}, bf16[64,4,8,128]{3,2,1,0:T(8,128)(2,1)}, u32[]{:S(2)}, u32[]{:S(2)}) collective-permute-start(bf16[64,4,8,128]{3,2,1,0:T(8,128)(2,1)} %collective-permute-done.4), channel_id=1, source_target_pairs={{0,4},{2,6},{4,0},{6,2},{8,12},{10,14},{12,8},{14,10},{16,20},{18,... | collective-permute-start | bytes 1572872 | tf_op jit(solution)/shard_map/ppermute | solution.py:20
  37.0 20.3 %copy-start.25 = (f32[4,8,128,64]{3,2,1,0:T(8,128)S(1)}, f32[4,8,128,64]{3,2,1,0:T(8,128)}, u32[]{:S(2)}) copy-start(f32[4,8,128,64]{3,2,1,0:T(8,128)} %get-tuple-element.766) | copy-start | bytes 3145732
  52.4 85.4 %collective-permute-start.3 = (bf16[1024,512]{1,0:T(8,128)(2,1)}, bf16[1024,512]{1,0:T(8,128)(2,1)}, u32[]{:S(2)}, u32[]{:S(2)}) collective-permute-start(bf16[1024,512]{1,0:T(8,128)(2,1)} %maximum_select_fusion.1), channel_id=1, source_target_pairs={{0,16},{2,18},{4,20},{6,22},{8,24},{10,26},{12,28},{14,30},{16,0},... | collective-permute-start | bytes 3145736 | tf_op jit(solution)/shard_map/ppermute | solution.py:201
  55.9 33.7 %collective-permute-start.6 = (bf16[64,4,8,128]{3,2,1,0:T(8,128)(2,1)}, bf16[64,4,8,128]{3,2,1,0:T(8,128)(2,1)}, u32[]{:S(2)}, u32[]{:S(2)}) collective-permute-start(bf16[64,4,8,128]{3,2,1,0:T(8,128)(2,1)} %collective-permute-done.5), channel_id=1, source_target_pairs={{0,8},{2,10},{4,12},{6,14},{8,0},{10,2},{12,4},{14,6},{16,24},{18,... | collective-permute-start | bytes 1572872 | tf_op jit(solution)/shard_map/ppermute | solution.py:20
  59.1 34.9 %copy-start.14 = (f32[4,8,128,64]{3,2,1,0:T(8,128)S(1)}, f32[4,8,128,64]{3,2,1,0:T(8,128)}, u32[]{:S(2)}) copy-start(f32[4,8,128,64]{3,2,1,0:T(8,128)} %copy-done.13) | copy-start | bytes 3145732
  61.0 33.8 %copy-start.27 = (bf16[8,8,32,128]{3,1,2,0:T(8,128)(2,1)S(1)}, bf16[8,8,32,128]{3,1,2,0:T(8,128)(2,1)}, u32[]{:S(2)}) copy-start(bf16[8,8,32,128]{3,1,2,0:T(8,128)(2,1)} %get-tuple-element.765) | copy-start | bytes 1572868
  89.6 69.9 %collective-permute-start.7 = (bf16[64,4,8,128]{3,2,1,0:T(8,128)(2,1)}, bf16[64,4,8,128]{3,2,1,0:T(8,128)(2,1)}, u32[]{:S(2)}, u32[]{:S(2)}) collective-permute-start(bf16[64,4,8,128]{3,2,1,0:T(8,128)(2,1)} %collective-permute-done.6), channel_id=1, source_target_pairs={{0,16},{2,18},{4,20},{6,22},{8,24},{10,26},{12,28},{14,30},{16,0},... | collective-permute-start | bytes 1572872 | tf_op jit(solution)/shard_map/ppermute | solution.py:20
  361.6 70.9 %collective-permute-start.8 = (bf16[4,8,64,128]{3,2,1,0:T(8,128)(2,1)}, bf16[4,8,64,128]{3,2,1,0:T(8,128)(2,1)S(1)}, u32[]{:S(2)}, u32[]{:S(2)}) collective-permute-start(bf16[4,8,64,128]{3,2,1,0:T(8,128)(2,1)} %divide_convert_fusion), channel_id=1, source_target_pairs={{0,2},{2,0},{4,6},{6,4},{8,10},{10,8},{12,14},{14,12},{16,18},{18,... | collective-permute-start | bytes 1572872 | tf_op jit(solution)/shard_map/ppermute | solution.py:20
  432.5 14.2 %collective-permute-start.9 = (bf16[4,8,64,128]{3,2,1,0:T(8,128)(2,1)S(1)}, bf16[4,8,64,128]{3,2,1,0:T(8,128)(2,1)S(1)}, u32[]{:S(2)}, u32[]{:S(2)}) collective-permute-start(bf16[4,8,64,128]{3,2,1,0:T(8,128)(2,1)S(1)} %collective-permute-done.8), channel_id=1, source_target_pairs={{0,4},{2,6},{4,0},{6,2},{8,12},{10,14},{12,8},{14,10},{16,20},{18,... | collective-permute-start | bytes 1572872 | tf_op jit(solution)/shard_map/ppermute | solution.py:20
  437.2 9.5 %copy-start.21 = (bf16[16,8,32,128]{3,2,1,0:T(8,128)(2,1)S(1)}, bf16[16,8,32,128]{3,2,1,0:T(8,128)(2,1)}, u32[]{:S(2)}) copy-start(bf16[16,8,32,128]{3,2,1,0:T(8,128)(2,1)} %copy-done.20) | copy-start | bytes 3145732
  437.2 9.5 %copy-start.31 = (bf16[128,4,128]{2,0,1:T(8,128)(2,1)S(1)}, bf16[128,4,128]{2,0,1:T(8,128)(2,1)}, u32[]{:S(2)}) copy-start(bf16[128,4,128]{2,0,1:T(8,128)(2,1)} %copy.128) | copy-start | bytes 393220
  446.7 13.4 %collective-permute-start.10 = (bf16[4,8,64,128]{3,2,1,0:T(8,128)(2,1)S(1)}, bf16[4,8,64,128]{3,2,1,0:T(8,128)(2,1)S(1)}, u32[]{:S(2)}, u32[]{:S(2)}) collective-permute-start(bf16[4,8,64,128]{3,2,1,0:T(8,128)(2,1)S(1)} %collective-permute-done.9), channel_id=1, source_target_pairs={{0,8},{2,10},{4,12},{6,14},{8,0},{10,2},{12,4},{14,6},{16,24},{18,... | collective-permute-start | bytes 1572872 | tf_op jit(solution)/shard_map/ppermute | solution.py:20
  449.0 12.4 %copy-start.29 = (bf16[128,4,128]{2,0,1:T(8,128)(2,1)S(1)}, bf16[128,4,128]{2,0,1:T(8,128)(2,1)}, u32[]{:S(2)}) copy-start(bf16[128,4,128]{2,0,1:T(8,128)(2,1)} %copy.139) | copy-start | bytes 393220
  460.1 24.6 %collective-permute-start.11 = (bf16[4,8,64,128]{3,2,1,0:T(8,128)(2,1)S(1)}, bf16[4,8,64,128]{3,2,1,0:T(8,128)(2,1)S(1)}, u32[]{:S(2)}, u32[]{:S(2)}) collective-permute-start(bf16[4,8,64,128]{3,2,1,0:T(8,128)(2,1)S(1)} %collective-permute-done.10), channel_id=1, source_target_pairs={{0,16},{2,18},{4,20},{6,22},{8,24},{10,26},{12,28},{14,30},{16,0},... | collective-permute-start | bytes 1572872 | tf_op jit(solution)/shard_map/ppermute | solution.py:20
  461.4 24.3 %copy-start.2 = (f32[4,8,128,128]{3,2,1,0:T(8,128)S(1)}, f32[4,8,128,128]{3,2,1,0:T(8,128)}, u32[]{:S(2)}) copy-start(f32[4,8,128,128]{3,2,1,0:T(8,128)} %custom-call) | copy-start | bytes 6291460
  534.8 12.1 %copy-start.3 = (f32[4,8,128,128]{3,2,1,0:T(8,128)}, f32[4,8,128,128]{3,2,1,0:T(8,128)S(1)}, u32[]{:S(2)}) copy-start(f32[4,8,128,128]{3,2,1,0:T(8,128)S(1)} %get-tuple-element.496) | copy-start | bytes 6291460
  552.9 267.9 %all-reduce.3.cloned.1.call-start = ((), (), s32[]{:S(2)}) async-start(), calls=%async_computation.1 | async-start | bytes 2097152 | tf_op jit(solution)/shard_map/psum | solution.py:310
  553.4 26.2 %copy-start.11 = (f32[4,8,192,64]{3,2,1,0:T(8,128)S(1)}, f32[4,8,192,64]{3,2,1,0:T(8,128)}, u32[]{:S(2)}) copy-start(f32[4,8,192,64]{3,2,1,0:T(8,128)} %copy-done.10) | copy-start | bytes 4718596
  579.6 7.9 copy-start.12
  579.6 7.9 copy-start.4
  678.0 38.6 %copy-start.24 = (bf16[128,512]{0,1:T(8,128)(2,1)S(1)}, bf16[128,512]{0,1:T(8,128)(2,1)}, u32[]{:S(2)}) copy-start(bf16[128,512]{0,1:T(8,128)(2,1)} %copy-done.23) | copy-start | bytes 393220
  770.1 53.1 %copy-start.1 = (bf16[32,128,64]{1,2,0:T(8,128)(2,1)S(1)}, bf16[32,128,64]{1,2,0:T(8,128)(2,1)}, u32[]{:S(2)}) copy-start(bf16[32,128,64]{1,2,0:T(8,128)(2,1)} %param.21) | copy-start | bytes 1572868
  (22 other events, 92.9 us)
Sparse Core Ops, SparseCore 0:
  10.2 73.5 all-gather.7
  85.9 151.4 all-gather.9
  553.1 124.8 all-gather.11
  729.4 91.4 all-reduce.2
